TPU v7x, 256 devices: a whole 4x4x8 slice. The times are simulated.
256 devices in a mesh: dp: 32 (over x, z_hi, core), expert: 8 (over y, z_lo).
Axes of the slice: x: 4, y: 4, z: 8 (z_hi: 4, z_lo: 2; z = z_hi * 2 + z_lo), core: 2. Of those that a mesh axis runs over, the one named last changes fastest.
Arguments:
- tokens: bfloat16 [73728, 2048], P(('dp', 'expert')), may hold values from -24 to 24
- expert_ids: int32 [73728, 8], P(('dp', 'expert')), may hold values from 0 to 127, all different within a row
- gates: float32 [73728, 8], P(('dp', 'expert')), may hold values from 0.05 to 1
- cotangent: bfloat16 [73728, 2048], P(('dp', 'expert')), may hold values from -1.25 to 1.25
- gate_weight: bfloat16 [8, 2048, 768], P('expert'), may hold values from -0.125 to 0.125
- up_weight: bfloat16 [8, 2048, 768], P('expert'), may hold values from -0.125 to 0.125
- down_weight: bfloat16 [8, 2048, 768], P('expert'), may hold values from -0.21875 to 0.21875
- block_masks: int32 [8, 3, 16, 6], P('expert'), may hold values 0 or 1
Outputs:
- combined: bfloat16 [73728, 2048], P(('dp', 'expert'))
- grad_gate: float32 [8, 2048, 768], P('expert', 'dp')
- grad_up: float32 [8, 2048, 768], P('expert', 'dp')
- grad_down: float32 [8, 2048, 768], P('expert', 'dp')
Inputs may be any that keep to these rules, and one draw needn't show every extreme that they name: `expert_ids`: each row names 8 different experts.
All inputs are finite; a program needn't handle non-finite values. No bound on the sum of `block_masks` on one device may be relied on, other than what follows from the above.
Results may differ from a plain program's by a relative error of at most 0.014.
Values may be sent and summed in bfloat16 or wider, within the bound.
A program may use at most 128 MiB of HBM per device.

v0:
```python
import functools

import jax
import jax.numpy as jnp
from jax import lax
from jax.experimental import pallas as pl
from jax.experimental.pallas import tpu as pltpu
from jax.sharding import PartitionSpec as P

MESH = pl.DeviceIdType.MESH
BF = jnp.bfloat16
F32 = jnp.float32
CAP = 18
E = 8
T = 288
TM = 144
D = 2048
FF = 768
BLK = 128
NB = 18
ROWS = 16
BUCKETS = (12, 13, 14, 18)
VMEM_LIMIT = 61900000


def nn(a, b):
    return jnp.dot(a, b, preferred_element_type=F32)


def nt(a, b):
    return lax.dot_general(a, b, (((1,), (1,)), ((), ())), preferred_element_type=F32)


def iota(shape, dim):
    return lax.broadcasted_iota(jnp.int32, shape, dim)


def flag(cond):
    return jnp.where(cond, 1.0, 0.0).astype(BF)


def act_kernel(
    tok_h, ids_ref, gat_ref, cot_h, wg_h, wu_h, wd_h, msk_ref,
    x_out, y_out, acts, rm, rr, wt, tbl_h, pick_ref,
    tok, cot, wg, wu, wd, sel, wsel, xs, xsr, ys, ysr, xr, xrr, yr, yrr,
    rem, g, u, mx, cells, tbl, cbuf, crec,
    lsem, osem, ssem, rsem,
):
    dp = lax.axis_index("dp")
    me = lax.axis_index("expert")

    loads = [
        pltpu.make_async_copy(tok_h, tok, lsem.at[0]),
        pltpu.make_async_copy(cot_h, cot, lsem.at[1]),
        pltpu.make_async_copy(wg_h, wg, lsem.at[2]),
        pltpu.make_async_copy(wu_h, wu, lsem.at[3]),
        pltpu.make_async_copy(wd_h, wd, lsem.at[4]),
    ]
    for load in loads:
        load.start()

    barrier = pltpu.get_barrier_semaphore()
    for k in range(1, E):
        pl.semaphore_signal(
            barrier, inc=1, device_id=(dp, lax.rem(me + k, E)), device_id_type=MESH
        )

    ids_t = ids_ref[...]
    gat_t = gat_ref[...].astype(BF).astype(F32)
    sub = iota((E, T), 0)
    hit = jnp.zeros((E, T), F32)
    gw = jnp.zeros((E, T), F32)
    for e in range(E):
        same = ids_t == e
        hit = jnp.where(
            sub == e, jnp.sum(jnp.where(same, 1.0, 0.0), axis=0, keepdims=True), hit
        )
        gw = jnp.where(
            sub == e, jnp.sum(jnp.where(same, gat_t, 0.0), axis=0, keepdims=True), gw
        )
    t0 = iota((T, T), 0)
    t1 = iota((T, T), 1)
    earlier = flag((t0 < t1) & ((t0 < TM) == (t1 < TM)))
    before = nn(hit.astype(BF), earlier)
    lane = iota((E, T), 1)
    kept = (hit > 0.0) & (before < float(CAP))
    slot = jnp.where(kept, before + jnp.where(lane < TM, 0.0, float(CAP)), -1.0)
    row8 = iota((T, E), 0)
    owner = jnp.where(row8 < 256, row8 // 32, (row8 - 256) // 4)
    spread = flag(owner == iota((T, E), 1))
    slot_rows = nn(spread, slot.astype(BF))
    want = jnp.where(t0 < 256, t0 % 32, 32 + (t0 - 256) % 4).astype(F32)
    chosen = slot_rows == want
    sel[...] = flag(chosen)

    def dispatch(matrix, source, main, tail):
        for n in range(2):
            cols = slice(1024 * n, 1024 * n + 1024)
            v = nn(matrix[...], source[:, cols])
            main[:, cols] = v[:256].astype(BF)
            for e in range(E):
                tail[e, :, cols] = v[256 + 4 * e : 260 + 4 * e].astype(BF)

    def moves(main, tail, main_to, tail_to, kind):
        out = []
        for k in range(1, E):
            to = lax.rem(me + k, E)
            out.append(
                pltpu.make_async_remote_copy(
                    src_ref=main.at[pl.ds(pl.multiple_of(to * 32, 32), 32)],
                    dst_ref=main_to.at[pl.ds(pl.multiple_of(me * 32, 32), 32)],
                    send_sem=ssem.at[kind, k],
                    recv_sem=rsem.at[kind, k],
                    device_id=(dp, to),
                    device_id_type=MESH,
                )
            )
            out.append(
                pltpu.make_async_remote_copy(
                    src_ref=tail.at[to],
                    dst_ref=tail_to.at[me],
                    send_sem=ssem.at[kind + 1, k],
                    recv_sem=rsem.at[kind + 1, k],
                    device_id=(dp, to),
                    device_id_type=MESH,
                )
            )
        own = [
            pltpu.make_async_copy(
                main.at[pl.ds(pl.multiple_of(me * 32, 32), 32)],
                main_to.at[pl.ds(pl.multiple_of(me * 32, 32), 32)],
                lsem.at[5 + kind],
            ),
            pltpu.make_async_copy(tail.at[me], tail_to.at[me], lsem.at[6 + kind]),
        ]
        return out, own

    def merge(main_to, tail_to):
        for e in range(E):
            rem[4 * e : 4 * e + 4, :] = tail_to[e].astype(F32)
        main_to[256:288, :] = rem[...].astype(BF)

    loads[0].wait()
    dispatch(sel, tok, xs, xsr)
    pl.semaphore_wait(barrier, E - 1)
    x_moves, x_own = moves(xs, xsr, xr, xrr, 0)
    for move in x_moves + x_own:
        move.start()
    gw_rows = nn(spread, gw.astype(BF))
    wsel[...] = jnp.where(chosen, gw_rows, 0.0).astype(BF)
    loads[1].wait()
    dispatch(wsel, cot, ys, ysr)
    y_moves, y_own = moves(ys, ysr, yr, yrr, 2)
    for move in y_moves + y_own:
        move.start()

    widths = (ROWS, BLK)
    for i in range(NB):
        cells[i : i + 1, :] = msk_ref[i].astype(F32)
    place = flag(iota((NB, BLK), 0) == iota((NB, BLK), 1))
    m2 = lax.dot_general(
        cells[0:NB, :].astype(BF), place, (((0,), (0,)), ((), ())), preferred_element_type=F32
    )
    tri = flag(iota((BLK, BLK), 0) <= iota((BLK, BLK), 1))
    upto = nn(m2.astype(BF), tri)
    pos = upto - 1.0
    most = jnp.max(jnp.max(upto, axis=1, keepdims=True), axis=0, keepdims=True)
    cbuf[...] = jnp.broadcast_to(most, (8, BLK))
    order = jnp.zeros(widths, F32)
    cell = iota(widths, 1).astype(F32)
    for i in range(NB):
        here = (pos[:, i : i + 1] == cell) & (m2[:, i : i + 1] > 0.0)
        order = order + jnp.where(here, float(i), 0.0)
    tbl[0:16, :] = order.astype(jnp.int32)
    tbl[16:32, :] = jnp.maximum(pos, 0.0).astype(jnp.int32)
    tbl[32:48, :] = m2.astype(jnp.int32)
    c_moves = []
    for k in range(1, E):
        to = lax.rem(me + k, E)
        c_moves.append(
            pltpu.make_async_remote_copy(
                src_ref=cbuf,
                dst_ref=crec.at[k],
                send_sem=ssem.at[4, k],
                recv_sem=rsem.at[4, k],
                device_id=(dp, to),
                device_id_type=MESH,
            )
        )
    for move in c_moves:
        move.start()

    for mat in range(3):
        lift = flag(iota((BLK, FF), 1) // BLK + 6 * mat == iota((BLK, FF), 0))
        mx[16 * mat : 16 * mat + 16, :] = nn(m2.astype(BF), lift)
    for load in loads[2:]:
        load.wait()

    def prune(r, carry):
        rows = pl.ds(pl.multiple_of(r * BLK, BLK), BLK)
        for mat, w in enumerate((wg, wu, wd)):
            w[rows, :] = w[rows, :] * mx[pl.ds(16 * mat + r, 1), :].astype(BF)
        return carry

    lax.fori_loop(0, ROWS, prune, 0)
    eye = flag(iota((T, T), 0) == iota((T, T), 1))
    wt[...] = nt(eye, wsel[...]).astype(BF)

    put = pltpu.make_async_copy(tbl, tbl_h, osem)
    put.start()

    for move in x_own:
        move.wait()
    for move in x_moves:
        move.wait_recv()
    merge(xr, xrr)
    for n in range(3):
        cols = slice(256 * n, 256 * n + 256)
        gv = nn(xr[...], wg[:, cols])
        uv = nn(xr[...], wu[:, cols])
        g[:, cols] = gv
        u[:, cols] = uv
        h_cols = slice(2 * FF + 256 * n, 2 * FF + 256 * n + 256)
        acts[:, h_cols] = (gv * jax.nn.sigmoid(gv) * uv).astype(BF)
    for n in range(8):
        cols = slice(256 * n, 256 * n + 256)
        v = nt(acts[:, 2 * FF : 3 * FF], wd[cols, :])
        rm[:, cols] = v[:256].astype(BF)
        for e in range(E):
            rr[e, :, cols] = v[256 + 4 * e : 260 + 4 * e].astype(BF)
    x_out[...] = xr[...]

    for move in c_moves:
        move.wait_recv()
    top = cbuf[...]
    for k in range(1, E):
        top = jnp.maximum(top, crec[k])
    peak = top[0, 0]
    pick = jnp.int32(0)
    for cz in BUCKETS[:-1]:
        pick = pick + jnp.where(peak > float(cz), 1, 0).astype(jnp.int32)
    pick_ref[0] = pick

    for move in y_own:
        move.wait()
    for move in y_moves:
        move.wait_recv()
    merge(yr, yrr)
    for n in range(3):
        cols = slice(256 * n, 256 * n + 256)
        u_cols = slice(FF + 256 * n, FF + 256 * n + 256)
        dh = nn(yr[...], wd[:, cols])
        gv = g[:, cols]
        s = jax.nn.sigmoid(gv)
        ds = dh * s
        acts[:, cols] = (ds * u[:, cols] * (1.0 + gv * (1.0 - s))).astype(BF)
        acts[:, u_cols] = (ds * gv).astype(BF)
    y_out[...] = yr[...]
    for move in x_moves + y_moves + c_moves:
        move.wait_send()
    put.wait()


def grad_kernel(
    cz,
    x_ref, y_ref, acts, rm, rr, wt, tbl_h,
    com_h, g_ref,
    tbl, ret, rer, rem, com, blk,
    cs, cr, sm, ra, rb, fp, fm, zz, za, zb, gp, gm,
    lsem, ssem, rsem, csem, crsem, xsem, xrsem, zsem, zrsem,
):
    na = cz // 2
    nb = cz - na
    dp = lax.axis_index("dp")
    me = lax.axis_index("expert")
    x = dp // 8
    z = (dp // 2) % 4
    c = dp % 2

    def at(xx, zz_, cc):
        return ((xx * 4 + zz_) * 2 + cc, me)

    twin = at(x, z, 1 - c)
    xp = at((x + 1) % 4, z, c)
    xm = at((x + 3) % 4, z, c)
    zp = at(x, (z + 1) % 4, c)
    zm = at(x, (z + 3) % 4, c)

    def x_of(i):
        return (x + (2, 1, 3, 0)[i]) % 4

    def z_of(q):
        step = jnp.where(q == 0, 2, jnp.where(q == 1, 1, jnp.where(q == 2, 3, 0)))
        return (z + step) % 4

    barrier = pltpu.get_barrier_semaphore()
    for peer in (twin, xp, xm, zp, zm):
        pl.semaphore_signal(barrier, inc=1, device_id=peer, device_id_type=MESH)
    for k in range(1, E):
        pl.semaphore_signal(
            barrier, inc=1, device_id=(dp, lax.rem(me + k, E)), device_id_type=MESH
        )

    loads = [
        pltpu.make_async_copy(
            rm.at[pl.ds(pl.multiple_of(me * 32, 32), 32)],
            ret.at[pl.ds(pl.multiple_of(me * 32, 32), 32)],
            lsem.at[2],
        ),
        pltpu.make_async_copy(rr.at[me], rer.at[me], lsem.at[3]),
    ]
    tables = pltpu.make_async_copy(tbl_h, tbl, lsem.at[5])
    tables.start()

    r_moves = []
    for k in range(1, E):
        to = lax.rem(me + k, E)
        r_moves.append(
            pltpu.make_async_remote_copy(
                src_ref=rm.at[pl.ds(pl.multiple_of(to * 32, 32), 32)],
                dst_ref=ret.at[pl.ds(pl.multiple_of(me * 32, 32), 32)],
                send_sem=ssem.at[0, k],
                recv_sem=rsem.at[0, k],
                device_id=(dp, to),
                device_id_type=MESH,
            )
        )
        r_moves.append(
            pltpu.make_async_remote_copy(
                src_ref=rr.at[to],
                dst_ref=rer.at[me],
                send_sem=ssem.at[1, k],
                recv_sem=rsem.at[1, k],
                device_id=(dp, to),
                device_id_type=MESH,
            )
        )
    def core_move(t, i):
        s = t * 4 + i
        return pltpu.make_async_remote_copy(
            src_ref=cs.at[s], dst_ref=cr.at[s],
            send_sem=csem.at[s], recv_sem=crsem.at[s],
            device_id=twin, device_id_type=MESH,
        )

    def x_move(kind, t):
        src, dst, peer = (
            lambda: (sm.at[4 * t, pl.ds(0, na)], ra.at[t], xp),
            lambda: (sm.at[4 * t, pl.ds(na, nb)], rb.at[t], xm),
            lambda: (sm.at[4 * t + 1, pl.ds(na, nb)], fp.at[t, pl.ds(na, nb)], xp),
            lambda: (sm.at[4 * t + 2, pl.ds(0, na)], fm.at[t, pl.ds(0, na)], xm),
            lambda: (sm.at[4 * t + 1, pl.ds(0, na)], fp.at[t, pl.ds(0, na)], xp),
            lambda: (sm.at[4 * t + 2, pl.ds(na, nb)], fm.at[t, pl.ds(na, nb)], xm),
        )[kind]()
        return pltpu.make_async_remote_copy(
            src_ref=src, dst_ref=dst,
            send_sem=xsem.at[kind, t], recv_sem=xrsem.at[kind, t],
            device_id=peer, device_id_type=MESH,
        )

    def z_move(kind):
        src, dst, peer = (
            lambda: (zz.at[0, pl.ds(0, na)], za, zp),
            lambda: (zz.at[0, pl.ds(na, nb)], zb, zm),
            lambda: (zz.at[1, pl.ds(na, nb)], gp.at[pl.ds(na, nb)], zp),
            lambda: (zz.at[1, pl.ds(0, na)], gm.at[pl.ds(0, na)], zm),
            lambda: (zz.at[2, pl.ds(0, na)], gp.at[pl.ds(0, na)], zp),
            lambda: (zz.at[2, pl.ds(na, nb)], gm.at[pl.ds(na, nb)], zm),
        )[kind]()
        return pltpu.make_async_remote_copy(
            src_ref=src, dst_ref=dst,
            send_sem=zsem.at[kind], recv_sem=zrsem.at[kind],
            device_id=peer, device_id_type=MESH,
        )

    for load in loads:
        load.start()
    tables.wait()

    def wide(v):
        return v.astype(F32)

    def product(q, carry):
        cols = []
        for i in range(4):
            r = x_of(i) * 4 + z_of(q)
            cols.append(pl.ds(pl.multiple_of(r * BLK, BLK), BLK))
        for n in range(9):
            source = x_ref if n < 6 else y_ref
            v = lax.dot_general(
                jnp.concatenate([source[:, col] for col in cols], axis=1),
                acts[:, 256 * n : 256 * n + 256],
                (((0,), (0,)), ((), ())),
                preferred_element_type=F32,
            )
            for i in range(4):
                for h in range(2):
                    blk[q, i, 2 * n + h] = v[
                        BLK * i : BLK * i + BLK, BLK * h : BLK * h + BLK
                    ].astype(BF)
        return carry

    def round_trip(v, carry):
        lo = jnp.where(v == 0, 0, jnp.where(v == 1, 1, jnp.where(v == 2, 3, 4)))
        hi = jnp.where(v == 0, 1, jnp.where(v == 1, 3, 4))
        lax.fori_loop(lo, hi, product, 0)

        @pl.when(v == 0)
        def _():
            pl.semaphore_wait(barrier, 12)
            for move in r_moves:
                move.start()

        @pl.when(v < 4)
        def _():
            t = v
            q_lo = jnp.where(t == 1, 2, jnp.where(t == 2, 1, t))
            for i in range(4):
                s = 4 * t + i
                for j in range(cz):
                    q = q_lo if j < na else t
                    b = tbl[x_of(i) * 4 + z_of(q), j]
                    cs[s, j] = blk[q, i, b, pl.ds(pl.multiple_of(64 * (1 - c), 64), 64), :]
                    sm[s, j] = blk[q, i, b, pl.ds(pl.multiple_of(64 * c, 64), 64), :]
                core_move(t, i).start()

        @pl.when(v >= 2)
        def _():
            p = v - 2
            for kind in (2, 3, 4, 5):
                x_move(kind, p).wait_recv()
            for j in range(cz):
                zz[p, j] = (
                    wide(sm[4 * p + 3, j]) + wide(fp[p, j]) + wide(fm[p, j])
                ).astype(BF)

        @pl.when(v == 2)
        def _():
            z_move(0).start()
            z_move(1).start()

        @pl.when(v == 3)
        def _():
            z_move(2).start()
            z_move(3).start()

        @pl.when(v == 4)
        def _():
            z_move(0).wait_recv()
            for j in range(na):
                zz[2, j] = (wide(zz[2, j]) + wide(za[j])).astype(BF)
            z_move(4).start()
            z_move(1).wait_recv()
            for j in range(nb):
                zz[2, na + j] = (wide(zz[2, na + j]) + wide(zb[j])).astype(BF)
            z_move(5).start()

        @pl.when(v >= 1)
        def _():
            p = v - 1
            x_move(0, p).wait_recv()
            for j in range(na):
                sm[4 * p + 1, j] = (wide(sm[4 * p + 1, j]) + wide(ra[p, j])).astype(BF)
            x_move(4, p).start()
            x_move(1, p).wait_recv()
            for j in range(nb):
                sm[4 * p + 2, na + j] = (
                    wide(sm[4 * p + 2, na + j]) + wide(rb[p, j])
                ).astype(BF)
            x_move(5, p).start()

        @pl.when(v < 4)
        def _():
            t = v
            for i in range(4):
                s = 4 * t + i
                core_move(t, i).wait_recv()
                for j in range(cz):
                    sm[s, j] = (wide(sm[s, j]) + wide(cr[s, j])).astype(BF)
                if i == 0:
                    x_move(0, t).start()
                    x_move(1, t).start()
                if i == 1:
                    x_move(2, t).start()
                if i == 2:
                    x_move(3, t).start()

        return carry

    lax.fori_loop(0, 5, round_trip, 0)

    for load in loads:
        load.wait()
    for move in r_moves:
        move.wait_recv()
    for e in range(E):
        rem[4 * e : 4 * e + 4, :] = rer[e].astype(F32)
    ret[256:288, :] = rem[...].astype(BF)

    for n in range(4):
        cols = slice(512 * n, 512 * n + 512)
        com[:, cols] = nn(wt[...], ret[:, cols]).astype(BF)
    put = pltpu.make_async_copy(com, com_h, lsem.at[4])
    put.start()

    for kind in (2, 3, 4, 5):
        x_move(kind, 3).wait_recv()
        z_move(kind).wait_recv()
    r = x * 4 + z
    for i in range(NB):
        p = tbl[16 + r, i]
        m = tbl[32 + r, i].astype(F32)
        v = wide(sm[15, p]) + wide(fp[3, p]) + wide(fm[3, p]) + wide(gp[p]) + wide(gm[p])
        g_ref[i // 6, :, BLK * (i % 6) : BLK * (i % 6) + BLK] = v * m

    for move in r_moves:
        move.wait_send()

    def drain(t, carry):
        for i in range(4):
            core_move(t, i).wait_send()
        for kind in range(6):
            x_move(kind, t).wait_send()
        return carry

    lax.fori_loop(0, 4, drain, 0)
    for kind in range(6):
        z_move(kind).wait_send()
    put.wait()


def final_kernel(com_h, g_h, out_h, gg_h, gu_h, gd_h, com, grad, isem, osem):
    loads = [
        pltpu.make_async_copy(
            com_h.at[pl.ds(96 * k, 96)], com.at[pl.ds(96 * k, 96)], isem.at[k]
        )
        for k in range(3)
    ] + [pltpu.make_async_copy(g_h.at[k], grad.at[k], isem.at[3 + k]) for k in range(3)]
    puts = [
        pltpu.make_async_copy(
            com.at[pl.ds(96 * k, 96)], out_h.at[pl.ds(96 * k, 96)], osem.at[k]
        )
        for k in range(3)
    ] + [
        pltpu.make_async_copy(grad.at[k], (gg_h, gu_h, gd_h)[k], osem.at[3 + k])
        for k in range(3)
    ]
    for load in loads:
        load.start()
    for load, put in zip(loads, puts):
        load.wait()
        put.start()
    for put in puts:
        put.wait()


def body(tokens, expert_ids, gates, cotangent, gate_weight, up_weight, down_weight, block_masks):
    any_spec = pl.BlockSpec(memory_space=pltpu.HBM)
    vmem = pl.BlockSpec(memory_space=pltpu.VMEM)
    shape = jax.ShapeDtypeStruct
    dma = pltpu.SemaphoreType.DMA
    smem = pl.BlockSpec(memory_space=pltpu.SMEM)
    x, y, acts, rm, rr, wt, tbl, pick = pl.pallas_call(
        act_kernel,
        out_shape=[
            shape((T, D), BF),
            shape((T, D), BF),
            shape((T, 3 * FF), BF),
            shape((256, D), BF),
            shape((E, 4, D), BF),
            shape((T, T), BF),
            shape((48, BLK), jnp.int32),
            shape((1,), jnp.int32),
        ],
        in_specs=[any_spec, vmem, vmem] + [any_spec] * 4 + [vmem],
        out_specs=[vmem] * 6 + [any_spec, smem],
        scratch_shapes=[
            pltpu.VMEM((T, D), BF),
            pltpu.VMEM((T, D), BF),
            pltpu.VMEM((D, FF), BF),
            pltpu.VMEM((D, FF), BF),
            pltpu.VMEM((D, FF), BF),
            pltpu.VMEM((T, T), BF),
            pltpu.VMEM((T, T), BF),
            pltpu.VMEM((256, D), BF),
            pltpu.VMEM((E, 4, D), BF),
            pltpu.VMEM((256, D), BF),
            pltpu.VMEM((E, 4, D), BF),
            pltpu.VMEM((T, D), BF),
            pltpu.VMEM((E, 4, D), BF),
            pltpu.VMEM((T, D), BF),
            pltpu.VMEM((E, 4, D), BF),
            pltpu.VMEM((32, D), F32),
            pltpu.VMEM((T, FF), F32),
            pltpu.VMEM((T, FF), F32),
            pltpu.VMEM((48, FF), F32),
            pltpu.VMEM((24, ROWS), F32),
            pltpu.VMEM((48, BLK), jnp.int32),
            pltpu.VMEM((8, BLK), F32),
            pltpu.VMEM((E, 8, BLK), F32),
            dma((9,)),
            dma(()),
            dma((5, E)),
            dma((5, E)),
        ],
        compiler_params=pltpu.CompilerParams(
            collective_id=0, has_side_effects=True, vmem_limit_bytes=VMEM_LIMIT
        ),
        name="act",
    )(
        tokens, expert_ids.T, gates.T, cotangent,
        gate_weight[0], up_weight[0], down_weight[0],
        block_masks.transpose(1, 3, 0, 2).reshape(NB, 1, ROWS),
    )

    def grads(index, cz):
        na, nb = cz // 2, cz - cz // 2

        def buf(*lead):
            return pltpu.VMEM(lead + (64, BLK), BF)

        return pl.pallas_call(
            functools.partial(grad_kernel, cz),
            out_shape=[
                shape((T, D), BF),
                shape((3, 64, FF), F32),
            ],
            in_specs=[vmem] * 6 + [any_spec],
            out_specs=[any_spec, vmem],
            scratch_shapes=[
                pltpu.SMEM((48, BLK), jnp.int32),
                pltpu.VMEM((T, D), BF),
                pltpu.VMEM((E, 4, D), BF),
                pltpu.VMEM((32, D), F32),
                pltpu.VMEM((T, D), BF),
                pltpu.VMEM((4, 4, NB, BLK, BLK), BF),
                buf(16, cz), buf(16, cz), buf(16, cz),
                buf(4, na), buf(4, nb), buf(4, cz), buf(4, cz),
                buf(3, cz), buf(na), buf(nb), buf(cz), buf(cz),
                dma((6,)),
                dma((2, E)),
                dma((2, E)),
                dma((16,)),
                dma((16,)),
                dma((6, 4)),
                dma((6, 4)),
                dma((6,)),
                dma((6,)),
            ],
            compiler_params=pltpu.CompilerParams(
                collective_id=1 + index, has_side_effects=True, vmem_limit_bytes=VMEM_LIMIT
            ),
            name=f"grad{cz}",
        )

    combined, g3 = lax.switch(
        pick[0],
        [lambda *ops, f=grads(i, cz): tuple(f(*ops)) for i, cz in enumerate(BUCKETS)],
        x, y, acts, rm, rr, wt, tbl,
    )
    combined, gg, gu, gd = pl.pallas_call(
        final_kernel,
        out_shape=[shape((T, D), BF)] + [shape((64, FF), F32)] * 3,
        in_specs=[any_spec] * 2,
        out_specs=[any_spec] * 4,
        scratch_shapes=[
            pltpu.VMEM((T, D), BF),
            pltpu.VMEM((3, 64, FF), F32),
            dma((6,)),
            dma((6,)),
        ],
        name="final",
    )(combined, g3)
    return (combined, gg[None], gu[None], gd[None])


def solution(mesh):
    return jax.shard_map(
        body,
        mesh=mesh,
        in_specs=(
            P(("dp", "expert"), None),
            P(("dp", "expert"), None),
            P(("dp", "expert"), None),
            P(("dp", "expert"), None),
            P("expert", None, None),
            P("expert", None, None),
            P("expert", None, None),
            P("expert", None, None, None),
        ),
        out_specs=(
            P(("dp", "expert"), None),
            P("expert", "dp", None),
            P("expert", "dp", None),
            P("expert", "dp", None),
        ),
        check_vma=False,
    )
```

profile of v0, /device:TPU:1, one launch (start us, length us, event | category | flops | bytes accessed | tf_op | source)
XLA Modules:
  0.0 83.3 jit_solution(13008014666355760032)
XLA Ops:
  0.6 37.6 %act.1 = (bf16[288,2048]{1,0:T(8,128)(2,1)S(1)}, bf16[288,2048]{1,0:T(8,128)(2,1)S(1)}, bf16[288,2304]{1,0:T(8,128)(2,1)S(1)}, bf16[256,2048]{1,0:T(8,128)(2,1)S...) custom-call(bf16[288,2048]{1,0:T(8,128)(2,1)} %tok_h.1, ...), custom_call_target="tpu_custom_call" | custom-call | tf_op jit(solution)/shard_map/act/pallas_call | solution.py:563
  38.9 41.9 %conditional.1 = ((bf16[288,2048]{1,0:T(8,128)(2,1)}, f32[3,64,768]{2,1,0:T(8,128)})) conditional(s32[]{:T(128)} %bitcast.7, (bf16[288,2048]{1,0:T(8,128)(2,1)S(1)}, bf16[288,2048]{1,0:T(8,128)(2,1)S(1)}, bf16[288,2304]{1,0:T(8,128)(2,1)S(1)}, bf16[256,2048]{1,0:T(8,128)(2,1)S(1)}, bf16[8,4,2048]{2,1,0:T(4,128)(2,1)S(1)}, ...), branch_computations={%region_0.0_spmd, %region_1.0_spmd, %region_2.0_spmd, %region_3.0_... | conditional | bytes 8 | solution.py:656
  39.1 41.4 %grad13.1 = (bf16[288,2048]{1,0:T(8,128)(2,1)}, f32[3,64,768]{2,1,0:T(8,128)}) custom-call(bf16[288,2048]{1,0:T(8,128)(2,1)S(1)} %get-tuple-element.63.x_ref, bf16[288,2048]{1,0:T(8,128)(2,1)S(1)} %get-tuple-element.64.y_ref, bf16[288,2304]{1,0:T(8,128)(2,1)S(1)} %get-tuple-element.65.acts, bf16[256,2048]{1,0:T(8,128)(2,1)S(1)} %get-tuple-element.66.rm, ...), custom_call_target="tpu_custom_call" | custom-call | tf_op jit(solution)/shard_map/cond/branch_1_fun/grad13/pallas_call | solution.py:658
  80.8 2.3 %final.1 = (bf16[288,2048]{1,0:T(8,128)(2,1)}, f32[64,768]{1,0:T(8,128)}, f32[64,768]{1,0:T(8,128)}, f32[64,768]{1,0:T(8,128)}) custom-call(bf16[288,2048]{1,0:T(8,128)(2,1)} %get-tuple-element.110.com_h, f32[3,64,768]{2,1,0:T(8,128)} %get-tuple-element.111.g_h), custom_call_target="tpu_custom_call" | custom-call | tf_op jit(solution)/shard_map/final/pallas_call | solution.py:661
where the time goes:
time: 82.4 us; the launch traced here: 83.3 us
  Pallas kernels  81.4 us (99%)
  between operations  1.45 us (2%)
    pallas_call x1, Pallas kernels, body(): f(*ops)  41.4 us
    pallas_call x1, Pallas kernels, body(): pl.pallas_call(act_kernel, out_shape=[shape((T, D), BF), shape((T, D), BF...  37.6 us
    pallas_call x1, Pallas kernels, body(): pl.pallas_call(final_kernel, out_shape=[shape((T, D), BF)] + [shape((64,...  2.29 us

commit v1 on v0

--- a/solution.py
+++ b/solution.py
@@ -19,7 +19,8 @@
 BLK = 128
 NB = 18
 ROWS = 16
-BUCKETS = (12, 13, 14, 18)
+BUCKETS = ((13, 9, 18), (14, 11, 20), (16, 14, 24), (18, 24, 42))
+HEAD = 6
 VMEM_LIMIT = 61900000
 
 
@@ -164,16 +165,46 @@
     tri = flag(iota((BLK, BLK), 0) <= iota((BLK, BLK), 1))
     upto = nn(m2.astype(BF), tri)
     pos = upto - 1.0
-    most = jnp.max(jnp.max(upto, axis=1, keepdims=True), axis=0, keepdims=True)
-    cbuf[...] = jnp.broadcast_to(most, (8, BLK))
     order = jnp.zeros(widths, F32)
     cell = iota(widths, 1).astype(F32)
     for i in range(NB):
         here = (pos[:, i : i + 1] == cell) & (m2[:, i : i + 1] > 0.0)
         order = order + jnp.where(here, float(i), 0.0)
+    r_i = iota((ROWS, ROWS), 0)
+    r_j = iota((ROWS, ROWS), 1)
+    line = r_i // 4 == r_j // 4
+    before_z = flag(line & (r_j % 4 == (r_i + 3) % 4))
+    after_z = flag(line & (r_j % 4 == (r_i + 1) % 4))
+    count = jnp.broadcast_to(upto[:, BLK - 1 :], widths)
+    o_prev = nn(before_z, order.astype(BF))
+    o_next = nn(after_z, order.astype(BF))
+    c_prev = nn(before_z, count.astype(BF))
+    c_next = nn(after_z, count.astype(BF))
+    rest_prev = jnp.maximum(c_prev - float(HEAD), 0.0)
+    rest = rest_prev + jnp.maximum(c_next - float(HEAD), 0.0)
+    shift = flag(iota((BLK, BLK), 1) == iota((BLK, BLK), 0) + HEAD)
+    heads = jnp.where(
+        cell < float(HEAD),
+        o_prev + 36.0,
+        jnp.where(cell < float(2 * HEAD), nn(o_next.astype(BF), shift) + 18.0, 0.0),
+    )
+    tails = jnp.zeros(widths, F32)
+    for i in range(NB):
+        here = (cell == rest + float(i)) & (count > float(i))
+        tails = tails + jnp.where(here, order[:, i : i + 1] + 54.0, 0.0)
+    for i in range(HEAD, NB):
+        here = (cell == float(i - HEAD)) & (c_prev > float(i))
+        tails = tails + jnp.where(here, o_prev[:, i : i + 1] + 36.0, 0.0)
+        here = (cell == rest_prev + float(i - HEAD)) & (c_next > float(i))
+        tails = tails + jnp.where(here, o_next[:, i : i + 1] + 18.0, 0.0)
+    sizes = jnp.where(cell == 0.0, count, jnp.where(cell == 1.0, rest, rest + count))
+    cbuf[...] = jnp.broadcast_to(jnp.max(sizes, axis=0, keepdims=True), (8, BLK))
     tbl[0:16, :] = order.astype(jnp.int32)
-    tbl[16:32, :] = jnp.maximum(pos, 0.0).astype(jnp.int32)
-    tbl[32:48, :] = m2.astype(jnp.int32)
+    tbl[16:32, :] = heads.astype(jnp.int32)
+    tbl[32:48, :] = tails.astype(jnp.int32)
+    tbl[48:64, :] = jnp.maximum(pos, 0.0).astype(jnp.int32)
+    tbl[64:80, :] = m2.astype(jnp.int32)
+    tbl[80:96, :] = count.astype(jnp.int32)
     c_moves = []
     for k in range(1, E):
         to = lax.rem(me + k, E)
@@ -235,10 +266,12 @@
     top = cbuf[...]
     for k in range(1, E):
         top = jnp.maximum(top, crec[k])
-    peak = top[0, 0]
     pick = jnp.int32(0)
-    for cz in BUCKETS[:-1]:
-        pick = pick + jnp.where(peak > float(cz), 1, 0).astype(jnp.int32)
+    for bucket in BUCKETS[:-1]:
+        over = top[0, 0] > float(bucket[0])
+        for k in (1, 2):
+            over = over | (top[0, k] > float(bucket[k]))
+        pick = pick + jnp.where(over, 1, 0).astype(jnp.int32)
     pick_ref[0] = pick
 
     for move in y_own:
@@ -262,15 +295,17 @@
 
 
 def grad_kernel(
-    cz,
+    bucket,
     x_ref, y_ref, acts, rm, rr, wt, tbl_h,
     com_h, g_ref,
     tbl, ret, rer, rem, com, blk,
-    cs, cr, sm, ra, rb, fp, fm, zz, za, zb, gp, gm,
+    cs, cr, sm, ra, rb, fp, fm, zz, za, zb, gp, gm, zt, zu, fin,
     lsem, ssem, rsem, csem, crsem, xsem, xrsem, zsem, zrsem,
 ):
-    na = cz // 2
-    nb = cz - na
+    cz, k2, total = bucket
+    ks = (cz, 2 * HEAD, k2, total - k2)
+    km = max(ks)
+    tail = cz - HEAD
     dp = lax.axis_index("dp")
     me = lax.axis_index("expert")
     x = dp // 8
@@ -344,13 +379,14 @@
         )
 
     def x_move(kind, t):
+        low, high = pl.ds(0, HEAD), pl.ds(HEAD, ks[t] - HEAD)
         src, dst, peer = (
-            lambda: (sm.at[4 * t, pl.ds(0, na)], ra.at[t], xp),
-            lambda: (sm.at[4 * t, pl.ds(na, nb)], rb.at[t], xm),
-            lambda: (sm.at[4 * t + 1, pl.ds(na, nb)], fp.at[t, pl.ds(na, nb)], xp),
-            lambda: (sm.at[4 * t + 2, pl.ds(0, na)], fm.at[t, pl.ds(0, na)], xm),
-            lambda: (sm.at[4 * t + 1, pl.ds(0, na)], fp.at[t, pl.ds(0, na)], xp),
-            lambda: (sm.at[4 * t + 2, pl.ds(na, nb)], fm.at[t, pl.ds(na, nb)], xm),
+            lambda: (sm.at[4 * t, low], ra.at[t], xp),
+            lambda: (sm.at[4 * t, high], rb.at[t, pl.ds(0, ks[t] - HEAD)], xm),
+            lambda: (sm.at[4 * t + 1, high], fp.at[t, high], xp),
+            lambda: (sm.at[4 * t + 2, low], fm.at[t, low], xm),
+            lambda: (sm.at[4 * t + 1, low], fp.at[t, low], xp),
+            lambda: (sm.at[4 * t + 2, high], fm.at[t, high], xm),
         )[kind]()
         return pltpu.make_async_remote_copy(
             src_ref=src, dst_ref=dst,
@@ -360,12 +396,12 @@
 
     def z_move(kind):
         src, dst, peer = (
-            lambda: (zz.at[0, pl.ds(0, na)], za, zp),
-            lambda: (zz.at[0, pl.ds(na, nb)], zb, zm),
-            lambda: (zz.at[1, pl.ds(na, nb)], gp.at[pl.ds(na, nb)], zp),
-            lambda: (zz.at[1, pl.ds(0, na)], gm.at[pl.ds(0, na)], zm),
-            lambda: (zz.at[2, pl.ds(0, na)], gp.at[pl.ds(0, na)], zp),
-            lambda: (zz.at[2, pl.ds(na, nb)], gm.at[pl.ds(na, nb)], zm),
+            lambda: (zz.at[0, pl.ds(0, HEAD)], za, zp),
+            lambda: (zz.at[0, pl.ds(HEAD, tail)], zb, zm),
+            lambda: (zz.at[1, pl.ds(0, HEAD)], gm.at[pl.ds(0, HEAD)], zm),
+            lambda: (zz.at[1, pl.ds(HEAD, HEAD)], gp.at[pl.ds(0, HEAD)], zp),
+            lambda: (zt, gp.at[pl.ds(HEAD, tail)], zp),
+            lambda: (zu, gm.at[pl.ds(HEAD, tail)], zm),
         )[kind]()
         return pltpu.make_async_remote_copy(
             src_ref=src, dst_ref=dst,
@@ -395,10 +431,26 @@
             )
             for i in range(4):
                 for h in range(2):
-                    blk[q, i, 2 * n + h] = v[
+                    blk[i, q * NB + 2 * n + h] = v[
                         BLK * i : BLK * i + BLK, BLK * h : BLK * h + BLK
                     ].astype(BF)
         return carry
+
+    def per_round(v, lag, action, rounds=4):
+        for t in range(rounds):
+
+            @pl.when(v == t + lag)
+            def _(t=t):
+                action(t)
+
+    def size_of(t):
+        return jnp.where(
+            t == 0, ks[0], jnp.where(t == 1, ks[1], jnp.where(t == 2, ks[2], ks[3]))
+        )
+
+    rest = [
+        jnp.maximum(tbl[80 + 4 * x + (z + step) % 4, 0] - HEAD, 0) for step in (3, 1)
+    ]
 
     def round_trip(v, carry):
         lo = jnp.where(v == 0, 0, jnp.where(v == 1, 1, jnp.where(v == 2, 3, 4)))
@@ -414,26 +466,39 @@
         @pl.when(v < 4)
         def _():
             t = v
-            q_lo = jnp.where(t == 1, 2, jnp.where(t == 2, 1, t))
+            base = jnp.where(t == 0, z_of(0), jnp.where(t == 1, 16 + z, 32 + z))
+            off = jnp.where(t == 3, k2, 0)
             for i in range(4):
                 s = 4 * t + i
-                for j in range(cz):
-                    q = q_lo if j < na else t
-                    b = tbl[x_of(i) * 4 + z_of(q), j]
-                    cs[s, j] = blk[q, i, b, pl.ds(pl.multiple_of(64 * (1 - c), 64), 64), :]
-                    sm[s, j] = blk[q, i, b, pl.ds(pl.multiple_of(64 * c, 64), 64), :]
+                for j in range(km):
+                    b = tbl[x_of(i) * 4 + base, off + j]
+                    cs[s, j] = blk[i, b, pl.ds(pl.multiple_of(64 * (1 - c), 64), 64), :]
+                    sm[s, j] = blk[i, b, pl.ds(pl.multiple_of(64 * c, 64), 64), :]
                 core_move(t, i).start()
 
+        def x_landed(t):
+            for kind in (2, 3, 4, 5):
+                x_move(kind, t).wait_recv()
+
+        per_round(v, 2, x_landed, 3)
+
         @pl.when(v >= 2)
         def _():
             p = v - 2
-            for kind in (2, 3, 4, 5):
-                x_move(kind, p).wait_recv()
-            for j in range(cz):
+
+            def add(j):
                 zz[p, j] = (
                     wide(sm[4 * p + 3, j]) + wide(fp[p, j]) + wide(fm[p, j])
                 ).astype(BF)
 
+            def step(j, carry):
+                add(j)
+                return carry
+
+            for j in range(HEAD):
+                add(j)
+            lax.fori_loop(HEAD, size_of(p), step, 0)
+
         @pl.when(v == 2)
         def _():
             z_move(0).start()
@@ -442,48 +507,68 @@
         @pl.when(v == 3)
         def _():
             z_move(2).start()
-            z_move(3).start()
 
         @pl.when(v == 4)
         def _():
-            z_move(0).wait_recv()
-            for j in range(na):
-                zz[2, j] = (wide(zz[2, j]) + wide(za[j])).astype(BF)
+            for j in range(tail):
+                zt[j] = zz[2, jnp.minimum(rest[0] + j, k2 - 1)]
             z_move(4).start()
             z_move(1).wait_recv()
-            for j in range(nb):
-                zz[2, na + j] = (wide(zz[2, na + j]) + wide(zb[j])).astype(BF)
+            for j in range(tail):
+                zu[j] = (wide(zz[2, j]) + wide(zb[j])).astype(BF)
             z_move(5).start()
 
+        per_round(v, 1, lambda t: x_move(0, t).wait_recv())
+
         @pl.when(v >= 1)
         def _():
             p = v - 1
-            x_move(0, p).wait_recv()
-            for j in range(na):
+            for j in range(HEAD):
                 sm[4 * p + 1, j] = (wide(sm[4 * p + 1, j]) + wide(ra[p, j])).astype(BF)
-            x_move(4, p).start()
-            x_move(1, p).wait_recv()
-            for j in range(nb):
-                sm[4 * p + 2, na + j] = (
-                    wide(sm[4 * p + 2, na + j]) + wide(rb[p, j])
+
+        def relay(t):
+            x_move(4, t).start()
+            x_move(1, t).wait_recv()
+
+        per_round(v, 1, relay)
+
+        @pl.when(v >= 1)
+        def _():
+            p = v - 1
+
+            def step(j, carry):
+                sm[4 * p + 2, HEAD + j] = (
+                    wide(sm[4 * p + 2, HEAD + j]) + wide(rb[p, j])
                 ).astype(BF)
-            x_move(5, p).start()
-
-        @pl.when(v < 4)
-        def _():
-            t = v
-            for i in range(4):
+                return carry
+
+            lax.fori_loop(0, size_of(p) - HEAD, step, 0)
+
+        per_round(v, 1, lambda t: x_move(5, t).start())
+
+        for i in range(4):
+
+            @pl.when(v < 4)
+            def _(i=i):
+                t = v
                 s = 4 * t + i
                 core_move(t, i).wait_recv()
-                for j in range(cz):
+                for j in range(km):
                     sm[s, j] = (wide(sm[s, j]) + wide(cr[s, j])).astype(BF)
-                if i == 0:
-                    x_move(0, t).start()
-                    x_move(1, t).start()
-                if i == 1:
-                    x_move(2, t).start()
-                if i == 2:
-                    x_move(3, t).start()
+
+            def send(t, i=i):
+                for kind in ((0, 1), (2,), (3,))[i]:
+                    x_move(kind, t).start()
+
+            if i < 3:
+                per_round(v, 0, send)
+
+        @pl.when(v == 3)
+        def _():
+            z_move(0).wait_recv()
+            for j in range(HEAD):
+                zz[1, HEAD + j] = (wide(zz[1, HEAD + j]) + wide(za[j])).astype(BF)
+            z_move(3).start()
 
         return carry
 
@@ -503,27 +588,31 @@
     put = pltpu.make_async_copy(com, com_h, lsem.at[4])
     put.start()
 
+    for j in range(k2):
+        fin[j] = wide(sm[11, j]) + wide(fp[2, j]) + wide(fm[2, j])
     for kind in (2, 3, 4, 5):
         x_move(kind, 3).wait_recv()
+    for j in range(total - k2):
+        fin[k2 + j] = wide(sm[15, j]) + wide(fp[3, j]) + wide(fm[3, j])
+    for kind in (2, 3, 4, 5):
         z_move(kind).wait_recv()
     r = x * 4 + z
     for i in range(NB):
-        p = tbl[16 + r, i]
-        m = tbl[32 + r, i].astype(F32)
-        v = wide(sm[15, p]) + wide(fp[3, p]) + wide(fm[3, p]) + wide(gp[p]) + wide(gm[p])
-        g_ref[i // 6, :, BLK * (i % 6) : BLK * (i % 6) + BLK] = v * m
+        p = tbl[48 + r, i]
+        m = tbl[64 + r, i].astype(F32)
+        f = jnp.minimum(rest[0] + rest[1] + p, total - 1)
+        g_ref[i // 6, :, BLK * (i % 6) : BLK * (i % 6) + BLK] = (
+            fin[f] + wide(gp[p]) + wide(gm[p])
+        ) * m
 
     for move in r_moves:
         move.wait_send()
 
-    def drain(t, carry):
+    for t in range(4):
         for i in range(4):
             core_move(t, i).wait_send()
         for kind in range(6):
             x_move(kind, t).wait_send()
-        return carry
-
-    lax.fori_loop(0, 4, drain, 0)
     for kind in range(6):
         z_move(kind).wait_send()
     put.wait()
@@ -569,7 +658,7 @@
             shape((256, D), BF),
             shape((E, 4, D), BF),
             shape((T, T), BF),
-            shape((48, BLK), jnp.int32),
+            shape((96, BLK), jnp.int32),
             shape((1,), jnp.int32),
         ],
         in_specs=[any_spec, vmem, vmem] + [any_spec] * 4 + [vmem],
@@ -595,7 +684,7 @@
             pltpu.VMEM((T, FF), F32),
             pltpu.VMEM((48, FF), F32),
             pltpu.VMEM((24, ROWS), F32),
-            pltpu.VMEM((48, BLK), jnp.int32),
+            pltpu.VMEM((96, BLK), jnp.int32),
             pltpu.VMEM((8, BLK), F32),
             pltpu.VMEM((E, 8, BLK), F32),
             dma((9,)),
@@ -613,14 +702,16 @@
         block_masks.transpose(1, 3, 0, 2).reshape(NB, 1, ROWS),
     )
 
-    def grads(index, cz):
-        na, nb = cz // 2, cz - cz // 2
+    def grads(index, bucket):
+        cz, k2, total = bucket
+        km = max(cz, 2 * HEAD, k2, total - k2)
+        tail = cz - HEAD
 
         def buf(*lead):
             return pltpu.VMEM(lead + (64, BLK), BF)
 
         return pl.pallas_call(
-            functools.partial(grad_kernel, cz),
+            functools.partial(grad_kernel, bucket),
             out_shape=[
                 shape((T, D), BF),
                 shape((3, 64, FF), F32),
@@ -628,15 +719,16 @@
             in_specs=[vmem] * 6 + [any_spec],
             out_specs=[any_spec, vmem],
             scratch_shapes=[
-                pltpu.SMEM((48, BLK), jnp.int32),
+                pltpu.SMEM((96, BLK), jnp.int32),
                 pltpu.VMEM((T, D), BF),
                 pltpu.VMEM((E, 4, D), BF),
                 pltpu.VMEM((32, D), F32),
                 pltpu.VMEM((T, D), BF),
-                pltpu.VMEM((4, 4, NB, BLK, BLK), BF),
-                buf(16, cz), buf(16, cz), buf(16, cz),
-                buf(4, na), buf(4, nb), buf(4, cz), buf(4, cz),
-                buf(3, cz), buf(na), buf(nb), buf(cz), buf(cz),
+                pltpu.VMEM((4, 4 * NB, BLK, BLK), BF),
+                buf(16, km), buf(16, km), buf(16, km),
+                buf(4, HEAD), buf(4, km - HEAD), buf(4, km), buf(4, km),
+                buf(3, km), buf(HEAD), buf(tail), buf(cz), buf(cz), buf(tail), buf(tail),
+                pltpu.VMEM((total, 64, BLK), F32),
                 dma((6,)),
                 dma((2, E)),
                 dma((2, E)),
@@ -650,12 +742,12 @@
             compiler_params=pltpu.CompilerParams(
                 collective_id=1 + index, has_side_effects=True, vmem_limit_bytes=VMEM_LIMIT
             ),
-            name=f"grad{cz}",
+            name=f"grad{index}",
         )
 
     combined, g3 = lax.switch(
         pick[0],
-        [lambda *ops, f=grads(i, cz): tuple(f(*ops)) for i, cz in enumerate(BUCKETS)],
+        [lambda *ops, f=grads(i, b): tuple(f(*ops)) for i, b in enumerate(BUCKETS)],
         x, y, acts, rm, rr, wt, tbl,
     )
     combined, gg, gu, gd = pl.pallas_call(

time: 82.4 us -> 85.5 us (1.038); the launches traced: 83.3 us -> 84.9 us
  Pallas kernels: 81.4 us -> 83.1 us
    pallas_call x1, Pallas kernels: 41.4 us -> 43 us  [body(): f(*ops)]
where the time goes in v1:
time: 85.5 us; the launch traced here: 84.9 us
  Pallas kernels  83.1 us (97%)
  between operations  1.45 us (2%)
    pallas_call x1, Pallas kernels, body(): f(*ops)  43 us
    pallas_call x1, Pallas kernels, body(): pl.pallas_call(act_kernel, out_shape=[shape((T, D), BF), shape((T, D), BF...  37.7 us
    pallas_call x1, Pallas kernels, body(): pl.pallas_call(final_kernel, out_shape=[shape((T, D), BF)] + [shape((64,...  2.29 us

profile of v1, /device:TPU:1, one launch (start us, length us, event | category | flops | bytes accessed | tf_op | source)
XLA Modules:
  0.0 84.9 jit_solution(16143058603464161233)
XLA Ops:
  0.6 37.7 %act.1 = (bf16[288,2048]{1,0:T(8,128)(2,1)S(1)}, bf16[288,2048]{1,0:T(8,128)(2,1)S(1)}, bf16[288,2304]{1,0:T(8,128)(2,1)S(1)}, bf16[256,2048]{1,0:T(8,128)(2,1)S...) custom-call(bf16[288,2048]{1,0:T(8,128)(2,1)} %tok_h.1, ...), custom_call_target="tpu_custom_call" | custom-call | tf_op jit(solution)/shard_map/act/pallas_call | solution.py:652
  39.0 43.5 %conditional.1 = ((bf16[288,2048]{1,0:T(8,128)(2,1)}, f32[3,64,768]{2,1,0:T(8,128)})) conditional(s32[]{:T(128)} %bitcast.7, (bf16[288,2048]{1,0:T(8,128)(2,1)S(1)}, bf16[288,2048]{1,0:T(8,128)(2,1)S(1)}, bf16[288,2304]{1,0:T(8,128)(2,1)S(1)}, bf16[256,2048]{1,0:T(8,128)(2,1)S(1)}, bf16[8,4,2048]{2,1,0:T(4,128)(2,1)S(1)}, ...), branch_computations={%region_0.0_spmd, %region_1.0_spmd, %region_2.0_spmd, %region_3.0_... | conditional | bytes 8 | solution.py:748
  39.0 43.0 %grad0.1 = (bf16[288,2048]{1,0:T(8,128)(2,1)}, f32[3,64,768]{2,1,0:T(8,128)}) custom-call(bf16[288,2048]{1,0:T(8,128)(2,1)S(1)} %get-tuple-element.56.x_ref, bf16[288,2048]{1,0:T(8,128)(2,1)S(1)} %get-tuple-element.57.y_ref, bf16[288,2304]{1,0:T(8,128)(2,1)S(1)} %get-tuple-element.58.acts, bf16[256,2048]{1,0:T(8,128)(2,1)S(1)} %get-tuple-element.59.rm, ...), custom_call_target="tpu_custom_call" | custom-call | tf_op jit(solution)/shard_map/cond/branch_0_fun/grad0/pallas_call | solution.py:750
  82.5 2.3 %final.1 = (bf16[288,2048]{1,0:T(8,128)(2,1)}, f32[64,768]{1,0:T(8,128)}, f32[64,768]{1,0:T(8,128)}, f32[64,768]{1,0:T(8,128)}) custom-call(bf16[288,2048]{1,0:T(8,128)(2,1)} %get-tuple-element.110.com_h, f32[3,64,768]{2,1,0:T(8,128)} %get-tuple-element.111.g_h), custom_call_target="tpu_custom_call" | custom-call | tf_op jit(solution)/shard_map/final/pallas_call | solution.py:753

commit v2 on v0

--- a/solution.py
+++ b/solution.py
@@ -19,7 +19,7 @@
 BLK = 128
 NB = 18
 ROWS = 16
-BUCKETS = (12, 13, 14, 18)
+BUCKETS = (11, 12, 13, 14, 15, 18)
 VMEM_LIMIT = 61900000
 
 
@@ -69,14 +69,10 @@
     gat_t = gat_ref[...].astype(BF).astype(F32)
     sub = iota((E, T), 0)
     hit = jnp.zeros((E, T), F32)
-    gw = jnp.zeros((E, T), F32)
     for e in range(E):
         same = ids_t == e
         hit = jnp.where(
             sub == e, jnp.sum(jnp.where(same, 1.0, 0.0), axis=0, keepdims=True), hit
-        )
-        gw = jnp.where(
-            sub == e, jnp.sum(jnp.where(same, gat_t, 0.0), axis=0, keepdims=True), gw
         )
     t0 = iota((T, T), 0)
     t1 = iota((T, T), 1)
@@ -146,6 +142,11 @@
     x_moves, x_own = moves(xs, xsr, xr, xrr, 0)
     for move in x_moves + x_own:
         move.start()
+    gw = jnp.zeros((E, T), F32)
+    for e in range(E):
+        gw = jnp.where(
+            sub == e, jnp.sum(jnp.where(ids_t == e, gat_t, 0.0), axis=0, keepdims=True), gw
+        )
     gw_rows = nn(spread, gw.astype(BF))
     wsel[...] = jnp.where(chosen, gw_rows, 0.0).astype(BF)
     loads[1].wait()
@@ -264,10 +265,10 @@
 def grad_kernel(
     cz,
     x_ref, y_ref, acts, rm, rr, wt, tbl_h,
-    com_h, g_ref,
-    tbl, ret, rer, rem, com, blk,
+    com_h, g_h,
+    tbl, ret, rer, rem, com, grad, blk,
     cs, cr, sm, ra, rb, fp, fm, zz, za, zb, gp, gm,
-    lsem, ssem, rsem, csem, crsem, xsem, xrsem, zsem, zrsem,
+    gsem, lsem, ssem, rsem, csem, crsem, xsem, xrsem, zsem, zrsem,
 ):
     na = cz // 2
     nb = cz - na
@@ -408,8 +409,6 @@
         @pl.when(v == 0)
         def _():
             pl.semaphore_wait(barrier, 12)
-            for move in r_moves:
-                move.start()
 
         @pl.when(v < 4)
         def _():
@@ -423,6 +422,11 @@
                     cs[s, j] = blk[q, i, b, pl.ds(pl.multiple_of(64 * (1 - c), 64), 64), :]
                     sm[s, j] = blk[q, i, b, pl.ds(pl.multiple_of(64 * c, 64), 64), :]
                 core_move(t, i).start()
+
+        @pl.when(v == 0)
+        def _():
+            for move in r_moves:
+                move.start()
 
         @pl.when(v >= 2)
         def _():
@@ -506,12 +510,17 @@
     for kind in (2, 3, 4, 5):
         x_move(kind, 3).wait_recv()
         z_move(kind).wait_recv()
+    def leave(k):
+        return pltpu.make_async_copy(grad.at[k], g_h.at[k], gsem.at[k])
+
     r = x * 4 + z
     for i in range(NB):
         p = tbl[16 + r, i]
         m = tbl[32 + r, i].astype(F32)
         v = wide(sm[15, p]) + wide(fp[3, p]) + wide(fm[3, p]) + wide(gp[p]) + wide(gm[p])
-        g_ref[i // 6, :, BLK * (i % 6) : BLK * (i % 6) + BLK] = v * m
+        grad[i // 6, :, BLK * (i % 6) : BLK * (i % 6) + BLK] = v * m
+        if i % 6 == 5:
+            leave(i // 6).start()
 
     for move in r_moves:
         move.wait_send()
@@ -527,6 +536,8 @@
     for kind in range(6):
         z_move(kind).wait_send()
     put.wait()
+    for k in range(3):
+        leave(k).wait()
 
 
 def final_kernel(com_h, g_h, out_h, gg_h, gu_h, gd_h, com, grad, isem, osem):
@@ -626,17 +637,19 @@
                 shape((3, 64, FF), F32),
             ],
             in_specs=[vmem] * 6 + [any_spec],
-            out_specs=[any_spec, vmem],
+            out_specs=[any_spec, any_spec],
             scratch_shapes=[
                 pltpu.SMEM((48, BLK), jnp.int32),
                 pltpu.VMEM((T, D), BF),
                 pltpu.VMEM((E, 4, D), BF),
                 pltpu.VMEM((32, D), F32),
                 pltpu.VMEM((T, D), BF),
+                pltpu.VMEM((3, 64, FF), F32),
                 pltpu.VMEM((4, 4, NB, BLK, BLK), BF),
                 buf(16, cz), buf(16, cz), buf(16, cz),
                 buf(4, na), buf(4, nb), buf(4, cz), buf(4, cz),
                 buf(3, cz), buf(na), buf(nb), buf(cz), buf(cz),
+                dma((3,)),
                 dma((6,)),
                 dma((2, E)),
                 dma((2, E)),

time: 82.4 us -> 82.1 us (level); the launches traced: 83.3 us -> 80.6 us
  Pallas kernels: 81.4 us -> 78.7 us
    pallas_call x1, Pallas kernels: 41.4 us -> 38.8 us  [body(): f(*ops)]
where the time goes in v2:
time: 82.1 us; the launch traced here: 80.6 us
  Pallas kernels  78.7 us (96%)
  between operations  1.45 us (2%)
    pallas_call x1, Pallas kernels, body(): f(*ops)  38.8 us
    pallas_call x1, Pallas kernels, body(): pl.pallas_call(act_kernel, out_shape=[shape((T, D), BF), shape((T, D), BF...  37.7 us
    pallas_call x1, Pallas kernels, body(): pl.pallas_call(final_kernel, out_shape=[shape((T, D), BF)] + [shape((64,...  2.29 us

profile of v2, /device:TPU:1, one launch (start us, length us, event | category | flops | bytes accessed | tf_op | source)
XLA Modules:
  0.0 80.6 jit_solution(15913435289619400390)
XLA Ops:
  0.6 37.7 %act.1 = (bf16[288,2048]{1,0:T(8,128)(2,1)S(1)}, bf16[288,2048]{1,0:T(8,128)(2,1)S(1)}, bf16[288,2304]{1,0:T(8,128)(2,1)S(1)}, bf16[256,2048]{1,0:T(8,128)(2,1)S...) custom-call(bf16[288,2048]{1,0:T(8,128)(2,1)} %tok_h.1, ...), custom_call_target="tpu_custom_call" | custom-call | tf_op jit(solution)/shard_map/act/pallas_call | solution.py:574
  38.9 39.2 %conditional.1 = ((bf16[288,2048]{1,0:T(8,128)(2,1)}, f32[3,64,768]{2,1,0:T(8,128)})) conditional(s32[]{:T(128)} %bitcast.7, (bf16[288,2048]{1,0:T(8,128)(2,1)S(1)}, bf16[288,2048]{1,0:T(8,128)(2,1)S(1)}, bf16[288,2304]{1,0:T(8,128)(2,1)S(1)}, bf16[256,2048]{1,0:T(8,128)(2,1)S(1)}, bf16[8,4,2048]{2,1,0:T(4,128)(2,1)S(1)}, ...), branch_computations={%region_0.0_spmd, %region_1.0_spmd, %region_2.0_spmd, %region_3.0_... | conditional | bytes 8 | solution.py:669
  39.1 38.8 %grad12.1 = (bf16[288,2048]{1,0:T(8,128)(2,1)}, f32[3,64,768]{2,1,0:T(8,128)}) custom-call(bf16[288,2048]{1,0:T(8,128)(2,1)S(1)} %get-tuple-element.91.x_ref, bf16[288,2048]{1,0:T(8,128)(2,1)S(1)} %get-tuple-element.92.y_ref, bf16[288,2304]{1,0:T(8,128)(2,1)S(1)} %get-tuple-element.93.acts, bf16[256,2048]{1,0:T(8,128)(2,1)S(1)} %get-tuple-element.94.rm, ...), custom_call_target="tpu_custom_call" | custom-call | tf_op jit(solution)/shard_map/cond/branch_1_fun/grad12/pallas_call | solution.py:671
  78.1 2.3 %final.1 = (bf16[288,2048]{1,0:T(8,128)(2,1)}, f32[64,768]{1,0:T(8,128)}, f32[64,768]{1,0:T(8,128)}, f32[64,768]{1,0:T(8,128)}) custom-call(bf16[288,2048]{1,0:T(8,128)(2,1)} %get-tuple-element.152.com_h, f32[3,64,768]{2,1,0:T(8,128)} %get-tuple-element.153.g_h), custom_call_target="tpu_custom_call" | custom-call | tf_op jit(solution)/shard_map/final/pallas_call | solution.py:674
